TPU v7x, 128 devices: a whole 4x4x4 slice. The times are simulated.
128 devices in a mesh: seq: 32 (over x, z, core), head: 4 (over y).
Axes of the slice: x: 4, y: 4, z: 4, core: 2. Of those that a mesh axis runs over, the one named last changes fastest.
Arguments:
- inputs: bfloat16 [32768, 6144], P('seq'), may hold values from -6 to 6
- query_vectors: bfloat16 [32768, 4096], P('seq', 'head')
- key_vectors: bfloat16 [32768, 4096], P('seq', 'head'), may hold values from -6 to 6
- value_weight: bfloat16 [6144, 4096], P('seq', 'head'), may hold values from -0.078125 to 0.078125
- log_decay: float32 [32, 32768], P('head', 'seq'), may hold values from -0.8 to 0
- doc_start: int32 [128], P('seq'), may hold values 0 or 1
- norm_gain: float32 [4096], P('head'), may hold values from 0.1 to 1.9
Outputs:
- attended: bfloat16 [32768, 4096], P('seq', 'head')
All inputs are finite; a program needn't handle non-finite values. No bound on the sum of `doc_start` on one device may be relied on, other than what follows from the above.
Results may differ from a plain program's by a relative error of at most 0.0053.
Values may be sent and summed in bfloat16 or wider, within the bound.
No kernel may reach another device: no remote copies, remote signals or barrier semaphores. Data moves between devices by JAX's collectives and lax.ppermute only.
A program may use at most 128 MiB of HBM per device.

v0:
```python
import jax
import jax.numpy as jnp
from jax import lax
from jax.sharding import PartitionSpec as P

SHARD_ATTN_PARTS = 32
E = 128
SPAN = 256


def per_device(inputs, query_vectors, key_vectors, value_weight, log_decay, doc_start, norm_gain):
    tok_rows = inputs.shape[0]
    width_out = value_weight.shape[1]
    head_count = width_out // E
    blocks = tok_rows // SPAN
    values = jnp.dot(
        inputs,
        lax.all_gather(value_weight, "seq", axis=0, tiled=True),
        preferred_element_type=jnp.float32,
    ).astype(jnp.bfloat16)
    query_blocks = query_vectors.reshape(blocks, SPAN, head_count, E)
    key_blocks = key_vectors.reshape(blocks, SPAN, head_count, E)
    value_blocks = values.reshape(blocks, SPAN, head_count, E)
    cumulative = jnp.cumsum(log_decay.reshape(head_count, blocks, SPAN), axis=2)
    cum_blocks = jnp.transpose(cumulative, (1, 0, 2))
    causal = lax.broadcasted_iota(jnp.int32, (SPAN, SPAN), 0) >= lax.broadcasted_iota(
        jnp.int32, (SPAN, SPAN), 1
    )
    scores = jnp.einsum(
        "cihe,cjhe->chij", query_blocks, key_blocks, preferred_element_type=jnp.float32
    )
    gaps = cum_blocks[:, :, :, None] - cum_blocks[:, :, None, :]
    weights = (scores * jnp.exp(jnp.where(causal[None, None], gaps, -1e30))).astype(jnp.bfloat16)
    inner = jnp.einsum("chij,cjhe->cihe", weights, value_blocks, preferred_element_type=jnp.float32)
    span_end = cumulative[:, :, -1]
    key_scale = jnp.transpose(jnp.exp(span_end[:, :, None] - cumulative), (1, 2, 0))[:, :, :, None]
    key_decayed = (key_blocks * key_scale).astype(jnp.bfloat16)
    updates = jnp.einsum(
        "cjhe,cjhf->chef", key_decayed, value_blocks, preferred_element_type=jnp.float32
    )
    survive = 1.0 - doc_start.astype(jnp.float32)
    local_memory = jnp.zeros((head_count, E, E), jnp.float32)
    carry_factor = jnp.ones((head_count,), jnp.float32)
    start_states = []
    start_factors = []
    for block in range(blocks):
        local_memory = local_memory * survive[block]
        carry_factor = carry_factor * survive[block]
        start_states.append(local_memory)
        start_factors.append(carry_factor)
        block_decay = jnp.exp(span_end[:, block])
        local_memory = block_decay[:, None, None] * local_memory + updates[block]
        carry_factor = carry_factor * block_decay
    all_factors, all_states = (
        lax.all_gather(carry_factor[None], "seq", axis=0, tiled=True),
        lax.all_gather(local_memory[None], "seq", axis=0, tiled=True),
    )
    position_now = lax.axis_index("seq")
    ranks = jnp.arange(all_factors.shape[0])
    earlier = (ranks < position_now)[:, None]
    factors_used = jnp.where(earlier, all_factors, 1.0)
    suffix = jnp.cumprod(factors_used[::-1], axis=0)[::-1]
    after = jnp.concatenate([suffix[1:], jnp.ones((1, head_count), jnp.float32)], axis=0)
    weights_sum = jnp.where(earlier, after, 0.0)
    incoming = jnp.einsum("nh,nhef->hef", weights_sum, all_states, precision=lax.Precision.HIGHEST)
    block_states = jnp.stack(start_factors)[:, :, None, None] * incoming[None] + jnp.stack(
        start_states
    )
    query_scale = jnp.transpose(jnp.exp(cumulative), (1, 2, 0))[:, :, :, None]
    query_decayed = query_blocks.astype(jnp.float32) * query_scale
    outer = jnp.einsum(
        "cihe,chef->cihf", query_decayed, block_states, precision=lax.Precision.HIGHEST
    )
    combined = (inner + outer).reshape(tok_rows, width_out)
    local_squares = jnp.sum(combined * combined, axis=1)
    square_total = lax.psum(local_squares, "head")
    mean_square = square_total / (SHARD_ATTN_PARTS * E)
    return (combined * lax.rsqrt(mean_square + 1e-06)[:, None] * norm_gain[None, :]).astype(
        jnp.bfloat16
    )


def solution(mesh):
    placed = (
        P("seq", None),
        P("seq", "head"),
        P("seq", "head"),
        P("seq", "head"),
        P("head", "seq"),
        P("seq"),
        P("head"),
    )
    return jax.shard_map(
        per_device, mesh=mesh, in_specs=placed, out_specs=P("seq", "head"), check_vma=False
    )
```

profile of v0, /device:TPU:0, one launch (start us, length us, event | category | flops | bytes accessed | tf_op | source)
XLA Modules:
  0.0 226.2 jit_solution(371942434578229823)
XLA Ops:
  6.5 0.7 all-gather.4.cloned.1.call-update
  7.3 0.8 copy.41
  8.1 2.3 reduce-window.6
  10.5 0.7 convert_subtract_fusion
  11.2 0.6 fusion.50
  12.5 3.5 %copy.56 = bf16[128,8,8,128]{3,2,1,0:T(8,128)(2,1)} copy(bf16[128,8,8,128]{3,1,2,0:T(8,128)(2,1)} %bitcast.91) | data formatting | bytes 4194304
  16.0 3.0 %copy.44 = bf16[4,256,8,128]{1,3,2,0:T(8,128)(2,1)S(1)} copy(bf16[4,256,8,128]{3,2,1,0:T(8,128)(2,1)} %bitcast.89) | data formatting | bytes 4194304 | tf_op jit(solution)/shard_map/reshape | solution.py:22
  19.4 55.7 %all-gather.4.cloned.1.call-done = bf16[6144,1024]{1,0:T(8,128)(2,1)} async-done(((bf16[192,1024]{1,0:T(8,128)(2,1)}), bf16[6144,1024]{1,0:T(8,128)(2,1)}) %all-gather.4.cloned.1.call-update) | async-done | bytes 12582928 | tf_op jit(solution)/shard_map/all_gather | solution.py:18
  75.1 17.4 %convert_bitcast_fusion = bf16[128,8,8,128]{3,1,2,0:T(8,128)(2,1)S(1)} fusion(bf16[1024,6144]{1,0:T(8,128)(2,1)} %param.7, bf16[6144,1024]{1,0:T(8,128)(2,1)} %all-gather.4.cloned.1.call-done), kind=kOutput, calls=%fused_computation.28 | convolution fusion | flops 12885950464 | bytes 27262976 | tf_op jit(solution)/shard_map/dot_general | solution.py:16
  92.5 0.6 copy.54
  93.1 0.8 fusion.16
  93.9 0.6 copy-done
  94.4 3.0 %slice_add_fusion = (f32[1,8,128,128]{3,2,1,0:T(8,128)}, f32[1,8,128,128]{3,2,1,0:T(8,128)S(1)}, f32[1,8,128,128]{3,2,1,0:T(8,128)S(1)}, f32[1,8,128,128]{3,2,1,0:T(8,128)}) fusion(f32[4,8,128,128]{3,2,1,0:T(8,128)S(1)} %fusion.16, f32[8]{0:T(128)S(1)} %get-tuple-element.18, f32[]{:T(128)} %bitcast.8, f32[8]{0:T(128)S(1)} %get-tuple-element.19, f32[]{:T(128)} %bitcast.6, ...), kind=kLoop, calls=%fused_computation.36 | loop fusion | flops 1310720 | bytes 4194444 | tf_op jit(solution)/shard_map/add | solution.py:52
  97.5 2.6 %fusion.36 = (f32[1,1,8]{2,1,0:T(1,128)S(1)}, f32[1,8]{1,0:T(1,128)S(1)}, f32[1,8]{1,0:T(1,128)S(1)}, f32[1,8]{1,0:T(1,128)S(1)}) fusion(f32[8,4]{0,1:T(4,128)S(1)} %slice_reduce_fusion.1, f32[]{:T(128)} %bitcast.8, f32[]{:T(128)} %bitcast.6, f32[]{:T(128)} %bitcast.3, f32[]{:T(128)} %bitcast.2), kind=kLoop, calls=%fused_computation.55 | loop fusion | flops 56 | bytes 272
  100.0 21.0 %all-gather = f32[32,1,8]{2,1,0:T(1,128)S(1)} all-gather(f32[1,1,8]{2,1,0:T(1,128)S(1)} %get-tuple-element.9), channel_id=1, replica_groups=mesh['seq'=32,'head'=4] {'seq'}, dimensions={0}, use_global_device_ids=true | all-gather | bytes 1056 | tf_op jit(solution)/shard_map/all_gather | solution.py:55
  121.3 0.7 pad.5.clone
  122.0 3.6 %copy.55 = bf16[128,8,8,128]{3,2,1,0:T(8,128)(2,1)} copy(bf16[128,8,8,128]{3,1,2,0:T(8,128)(2,1)} %bitcast.92) | data formatting | bytes 4194304
  125.7 6.5 %fusion.2 = f32[4,8,128,256]{3,2,1,0:T(8,128)} fusion(f32[4,8,256]{2,1,0:T(8,128)S(1)} %get-tuple-element.16, pred[256,256]{1,0:T(8,128)(4,1)S(1)} %iota_compare_fusion, bf16[4,256,8,128]{1,3,2,0:T(8,128)(2,1)S(1)} %copy.44, bf16[4,256,8,128]{3,2,1,0:T(8,128)(2,1)} %bitcast.86, bf16[4,256,8,128]{3,2,1,0:T(8,128)(2,1)} %bitcast.87), kind=kOutput, calls=%fused_computation.3 | convolution fusion | flops 1082130432 | bytes 10584064 | tf_op jit(solution)/shard_map/chij,cjhe->cihe/dot_general | solution.py:34
  132.2 37.6 %all-gather.6.cloned.1.call-done = f32[32,8,128,128]{3,2,1,0:T(8,128)} async-done(((f32[1,8,128,128]{3,2,1,0:T(8,128)}), f32[32,8,128,128]{3,2,1,0:T(8,128)}) %all-gather.6.cloned.1.call-update) | async-done | bytes 16777232 | tf_op jit(solution)/shard_map/all_gather | solution.py:56
  169.8 22.0 %fusion = f32[8,1,128,128]{3,1,2,0:T(1,128)S(1)} fusion(f32[32,8,1,1]{0,2,3,1:T(1,128)S(1)} %copy.49, f32[32,8,128,128]{3,2,1,0:T(8,128)} %all-gather.6.cloned.1.call-done), kind=kOutput, calls=%fused_computation | convolution fusion | flops 50331648 | bytes 17302528 | tf_op jit(solution)/shard_map/nh,nhef->hef/dot_general | solution.py:65
  191.8 7.6 %multiply_reduce_fusion = (f32[4,256]{1,0:T(4,128)S(1)}, f32[4,256,8,128]{1,3,2,0:T(8,128)}) fusion(f32[4,8,128,256]{3,2,1,0:T(8,128)S(1)} %copy-done.2, f32[4,256,8]{1,2,0:T(8,128)S(1)} %get-tuple-element.13, bf16[4,256,8,128]{3,2,1,0:T(8,128)(2,1)S(1)} %bitcast.88, f32[1,8,128,128]{3,2,1,0:T(8,128)S(1)} %get-tuple-element.6, ...), kind=kOutput, calls=%fused_computation.7 | convolution fusion | flops 1618476032 | bytes 12619920 | tf_op jit(solution)/shard_map/cihe,chef->cihf/dot_general | solution.py:71
  199.4 5.3 %copy.48 = f32[4,256,8,128]{3,2,1,0:T(8,128)} copy(f32[4,256,8,128]{1,3,2,0:T(8,128)} %get-tuple-element.26) | data formatting | bytes 8388608 | tf_op jit(solution)/shard_map/add | solution.py:74
  204.7 10.5 %psum.7 = f32[1024]{0:T(1024)S(1)} all-reduce(f32[1024]{0:T(1024)S(1)} %bitcast.97), channel_id=1, replica_groups=mesh['seq'=32,'head'=4] {'head'}, use_global_device_ids=true, to_apply=%region_4.5 | all-reduce | flops 1024 | bytes 8192 | tf_op jit(solution)/shard_map/psum | solution.py:76
  215.1 4.3 %fusion.4 = bf16[1024,1024]{1,0:T(8,128)(2,1)} fusion(f32[128,8,8,128]{3,2,1,0:T(8,128)} %bitcast.84, f32[1024]{0:T(1024)S(1)} %copy-done.4, f32[1024]{0:T(1024)S(1)} %add_rsqrt_fusion), kind=kLoop, calls=%fused_computation.6 | loop fusion | flops 3145728 | bytes 6299648 | tf_op jit(solution)/shard_map/convert_element_type | solution.py:78
  (31 shorter events, 1.0 us)
Async XLA Ops:
  6.5 68.5 %all-gather.4.cloned.1.call-start = ((), (), s32[]{:S(2)}) async-start(), calls=%async_computation | async-start | bytes 12976128 | tf_op jit(solution)/shard_map/all_gather | solution.py:18
  7.3 162.5 %all-gather.6.cloned.1.call-start = ((), (), s32[]{:S(2)}) async-start(), calls=%async_computation.1 | async-start | bytes 17301504 | tf_op jit(solution)/shard_map/all_gather | solution.py:56
  93.1 1.3 copy-start
  132.2 59.6 %copy-start.1 = (bf16[128,8,8,128]{3,2,1,0:T(8,128)(2,1)S(1)}, bf16[128,8,8,128]{3,2,1,0:T(8,128)(2,1)}, u32[]{:S(2)}) copy-start(bf16[128,8,8,128]{3,2,1,0:T(8,128)(2,1)} %copy.55) | copy-start | bytes 6291460
  169.8 22.0 %copy-start.2 = (f32[4,8,128,256]{3,2,1,0:T(8,128)S(1)}, f32[4,8,128,256]{3,2,1,0:T(8,128)}, u32[]{:S(2)}) copy-start(f32[4,8,128,256]{3,2,1,0:T(8,128)} %fusion.2) | copy-start | bytes 12582916
  169.8 22.0 %copy-start.3 = (f32[1,8,128,128]{3,2,1,0:T(8,128)S(1)}, f32[1,8,128,128]{3,2,1,0:T(8,128)}, u32[]{:S(2)}) copy-start(f32[1,8,128,128]{3,2,1,0:T(8,128)} %get-tuple-element.8) | copy-start | bytes 1572868
  199.4 15.7 %copy-start.4 = (f32[1024]{0:T(1024)S(1)}, f32[1024]{0:T(1024)}, u32[]{:S(2)}) copy-start(f32[1024]{0:T(1024)} %param.13) | copy-start | bytes 12292
Sparse Core Ops, SparseCore 0:
  9.6 65.4 all-gather.3
  97.6 72.1 all-gather.5
where the time goes:
time: 227 us; the launch traced here: 226 us
  waiting for transfers between devices  94 us (41%)
  matrix products  54.2 us (24%)
  blocking collectives  31.4 us (14%)
  local copies, waits for them, and re-layouts  19 us (8%)
  between operations  14.2 us (6%)
  other arithmetic  13.3 us (6%)
    all_gather x1, waiting for transfers between devices, per_device(): lax.all_gather(value_weight, 'seq', axis=0, tiled=True)  55.7 us
    all_gather x1, waiting for transfers between devices, per_device(): lax.all_gather(local_memory[None], 'seq', axis=0, tiled=True)  37.6 us
    dot_general x1, matrix products, per_device(): jnp.einsum('nh,nhef->hef', weights_sum, all_states, precision=lax.Precisi...  22 us
    all_gather x1, blocking collectives, per_device(): lax.all_gather(carry_factor[None], 'seq', axis=0, tiled=True)  21 us
    dot_general x1, matrix products, per_device(): jnp.dot(inputs, lax.all_gather(value_weight, 'seq', axis=0, tiled=True),...  17.4 us
    psum x1, blocking collectives, per_device(): square_total = lax.psum(local_squares, 'head')  10.5 us
    unnamed x14, local copies, waits for them, and re-layouts  8.29 us
    dot_general x1, matrix products, per_device(): jnp.einsum('cihe,chef->cihf', query_decayed, block_states, precision=lax....  7.58 us
  transfers between devices with their start and end apart: 2, of which 2 were waited for; matrix products, arithmetic and copies ran while one was open for 11% of the time, Pallas kernels for 0%

commit v1 on v0

--- a/solution.py
+++ b/solution.py
@@ -6,6 +6,11 @@
 SHARD_ATTN_PARTS = 32
 E = 128
 SPAN = 256
+
+
+def exchange_gather(block, name, along):
+    sent = jnp.stack([block] * lax.axis_size(name))
+    return jnp.concatenate(lax.all_to_all(sent, name, 0, 0), axis=along)
 
 
 def per_device(inputs, query_vectors, key_vectors, value_weight, log_decay, doc_start, norm_gain):
@@ -53,7 +58,7 @@
         carry_factor = carry_factor * block_decay
     all_factors, all_states = (
         lax.all_gather(carry_factor[None], "seq", axis=0, tiled=True),
-        lax.all_gather(local_memory[None], "seq", axis=0, tiled=True),
+        exchange_gather(local_memory[None], "seq", 0),
     )
     position_now = lax.axis_index("seq")
     ranks = jnp.arange(all_factors.shape[0])

time: 227 us -> 463 us (2.04)
  blocking collectives: 31.4 us -> 289 us
  waiting for transfers between devices: 94 us -> 56.5 us
  local copies, waits for them, and re-layouts: 19 us -> 26.8 us
  starting transfers between devices: 0.04 us -> 5.54 us
    all_gather x1, blocking collectives: 21 us -> 279 us  [per_device(): lax.all_gather(carry_factor[None], 'seq', axis=0, tiled=True)]
    all_gather x1 -> x0, waiting for transfers between devices: 37.6 us -> none  [per_device(): lax.all_gather(local_memory[None], 'seq', axis=0, tiled=True)]
    another operation x1 -> x2, local copies, waits for them, and re-layouts: 0.01 us -> 7.84 us  [the longest x1 7.84 us: exchange_gather(): sent = jnp.stack([block] * lax.axis_size(name))]
    all_to_all x0 -> x1, starting transfers between devices: none -> 5.54 us  [exchange_gather(): return jnp.concatenate(lax.all_to_all(sent, name, 0, 0), axis=along)]
  transfers between devices with their start and end apart: 2 -> 2, of which waited for: 2 -> 1; matrix products, arithmetic and copies ran while one was open for 11% -> 5% of each run, Pallas kernels for 0% -> 0%
where the time goes in v1:
time: 463 us; the launch traced here: 459 us
  blocking collectives  289 us (62%)
  waiting for transfers between devices  56.5 us (12%)
  matrix products  54.3 us (12%)
  local copies, waits for them, and re-layouts  26.8 us (6%)
  between operations  14.2 us (3%)
  other arithmetic  13 us (3%)
  starting transfers between devices  5.54 us (1%)
    all_gather x1, blocking collectives, per_device(): lax.all_gather(carry_factor[None], 'seq', axis=0, tiled=True)  279 us
    all_gather x1, waiting for transfers between devices, per_device(): lax.all_gather(value_weight, 'seq', axis=0, tiled=True)  55.8 us
    dot_general x1, matrix products, per_device(): jnp.einsum('nh,nhef->hef', weights_sum, all_states, precision=lax.Precisi...  22 us
    dot_general x1, matrix products, per_device(): jnp.dot(inputs, lax.all_gather(value_weight, 'seq', axis=0, tiled=True),...  17.4 us
    psum x1, blocking collectives, per_device(): square_total = lax.psum(local_squares, 'head')  10.5 us
  transfers between devices with their start and end apart: 2, of which 1 were waited for; matrix products, arithmetic and copies ran while one was open for 5% of the time, Pallas kernels for 0%

profile of v1, /device:TPU:0, one launch (start us, length us, event | category | flops | bytes accessed | tf_op | source)
XLA Modules:
  0.0 459.4 jit_solution(3480467400247969362)
XLA Ops:
  6.5 0.7 all-gather.3.cloned.1.call-update
  7.3 0.8 copy.41
  8.0 2.3 reduce-window.6
  10.5 0.7 convert_subtract_fusion
  11.1 0.7 fusion.51
  12.4 3.5 copy.56
  15.9 3.0 copy.44
  19.3 55.8 %all-gather.3.cloned.1.call-done = bf16[6144,1024]{1,0:T(8,128)(2,1)} async-done(((bf16[192,1024]{1,0:T(8,128)(2,1)}), bf16[6144,1024]{1,0:T(8,128)(2,1)}) %all-gather.3.cloned.1.call-update) | async-done | bytes 12582928 | tf_op jit(solution)/shard_map/all_gather | solution.py:23
  75.1 17.4 %convert_bitcast_fusion = bf16[128,8,8,128]{3,1,2,0:T(8,128)(2,1)S(1)} fusion(bf16[1024,6144]{1,0:T(8,128)(2,1)} %param.7, bf16[6144,1024]{1,0:T(8,128)(2,1)} %all-gather.3.cloned.1.call-done), kind=kOutput, calls=%fused_computation.28 | convolution fusion | flops 12885950464 | bytes 27262976 | tf_op jit(solution)/shard_map/dot_general | solution.py:21
  92.4 0.6 copy.54
  93.1 0.8 fusion.16
  94.4 2.8 fusion.33
  97.2 7.8 %stack.26 = f32[32,1,8,128,128]{4,3,2,1,0:T(8,128)} broadcast(f32[8,128,128]{2,1,0:T(8,128)S(1)} %get-tuple-element.5), dimensions={2,3,4} | broadcast | bytes 17301504 | tf_op jit(solution)/shard_map/stack | solution.py:12
  105.1 5.5 %all-to-all-start = ((f32[32,1,8,128,128]{4,3,2,1,0:T(8,128)}), f32[32,1,8,128,128]{4,3,2,1,0:T(8,128)}, u32[]{:S(2)}, u32[]{:S(2)}) async-start(f32[32,1,8,128,128]{4,3,2,1,0:T(8,128)} %stack.26), calls=%async_computation | async-start | bytes 33554432 | tf_op jit(solution)/shard_map/all_to_all | solution.py:13
  110.6 2.5 fusion.37
  113.1 278.6 %all-gather = f32[32,1,8]{2,1,0:T(1,128)S(1)} all-gather(f32[1,1,8]{2,1,0:T(1,128)S(1)} %get-tuple-element.9), channel_id=1, replica_groups=mesh['seq'=32,'head'=4] {'seq'}, dimensions={0}, use_global_device_ids=true | all-gather | bytes 1056 | tf_op jit(solution)/shard_map/all_gather | solution.py:60
  392.0 0.6 pad.5.clone
  392.6 3.5 copy.55
  396.3 6.6 %fusion.2 = f32[4,8,128,256]{3,2,1,0:T(8,128)} fusion(f32[4,8,256]{2,1,0:T(8,128)S(1)} %get-tuple-element.16, pred[256,256]{1,0:T(8,128)(4,1)S(1)} %iota_compare_fusion, bf16[4,256,8,128]{1,3,2,0:T(8,128)(2,1)S(1)} %copy.44, bf16[4,256,8,128]{3,2,1,0:T(8,128)(2,1)} %bitcast.89, bf16[4,256,8,128]{3,2,1,0:T(8,128)(2,1)} %bitcast.90), kind=kOutput, calls=%fused_computation.3 | convolution fusion | flops 1082130432 | bytes 10584064 | tf_op jit(solution)/shard_map/chij,cjhe->cihe/dot_general | solution.py:39
  402.9 22.0 %fusion = f32[8,1,128,128]{3,1,2,0:T(1,128)S(1)} fusion(f32[32,8,1,1]{0,2,3,1:T(1,128)S(1)} %copy.49, f32[32,8,128,128]{3,2,1,0:T(8,128)} %bitcast.19), kind=kOutput, calls=%fused_computation | convolution fusion | flops 50331648 | bytes 17302528 | tf_op jit(solution)/shard_map/nh,nhef->hef/dot_general | solution.py:70
  424.9 7.6 %multiply_reduce_fusion = (f32[4,256]{1,0:T(4,128)S(1)}, f32[4,256,8,128]{1,3,2,0:T(8,128)}) fusion(f32[4,8,128,256]{3,2,1,0:T(8,128)S(1)} %copy-done.2, f32[4,256,8]{1,2,0:T(8,128)S(1)} %get-tuple-element.13, bf16[4,256,8,128]{3,2,1,0:T(8,128)(2,1)S(1)} %bitcast.91, f32[1,8,128,128]{3,2,1,0:T(8,128)S(1)} %get-tuple-element.6, ...), kind=kOutput, calls=%fused_computation.7 | convolution fusion | flops 1618476032 | bytes 12619920 | tf_op jit(solution)/shard_map/cihe,chef->cihf/dot_general | solution.py:76
  432.5 5.3 %copy.48 = f32[4,256,8,128]{3,2,1,0:T(8,128)} copy(f32[4,256,8,128]{1,3,2,0:T(8,128)} %get-tuple-element.26) | data formatting | bytes 8388608 | tf_op jit(solution)/shard_map/add | solution.py:79
  437.8 10.5 %psum.7 = f32[1024]{0:T(1024)S(1)} all-reduce(f32[1024]{0:T(1024)S(1)} %bitcast.100), channel_id=1, replica_groups=mesh['seq'=32,'head'=4] {'head'}, use_global_device_ids=true, to_apply=%region_4.5 | all-reduce | flops 1024 | bytes 8192 | tf_op jit(solution)/shard_map/psum | solution.py:81
  448.2 4.3 fusion.4
  (31 shorter events, 1.5 us)
Async XLA Ops:
  6.5 68.5 %all-gather.3.cloned.1.call-start = ((), (), s32[]{:S(2)}) async-start(), calls=%async_computation.1 | async-start | bytes 12976128 | tf_op jit(solution)/shard_map/all_gather | solution.py:23
  93.1 1.3 copy-start
  105.1 297.8 %all-to-all-start = ((f32[32,1,8,128,128]{4,3,2,1,0:T(8,128)}), f32[32,1,8,128,128]{4,3,2,1,0:T(8,128)}, u32[]{:S(2)}, u32[]{:S(2)}) async-start(f32[32,1,8,128,128]{4,3,2,1,0:T(8,128)} %stack.26), calls=%async_computation | async-start | bytes 33554432 | tf_op jit(solution)/shard_map/all_to_all | solution.py:13
  402.9 22.0 %copy-start.1 = (bf16[128,8,8,128]{3,2,1,0:T(8,128)(2,1)S(1)}, bf16[128,8,8,128]{3,2,1,0:T(8,128)(2,1)}, u32[]{:S(2)}) copy-start(bf16[128,8,8,128]{3,2,1,0:T(8,128)(2,1)} %copy.55) | copy-start | bytes 6291460
  402.9 22.0 %copy-start.2 = (f32[4,8,128,256]{3,2,1,0:T(8,128)S(1)}, f32[4,8,128,256]{3,2,1,0:T(8,128)}, u32[]{:S(2)}) copy-start(f32[4,8,128,256]{3,2,1,0:T(8,128)} %fusion.2) | copy-start | bytes 12582916
  402.9 22.0 %copy-start.3 = (f32[1,8,128,128]{3,2,1,0:T(8,128)S(1)}, f32[1,8,128,128]{3,2,1,0:T(8,128)}, u32[]{:S(2)}) copy-start(f32[1,8,128,128]{3,2,1,0:T(8,128)} %get-tuple-element.8) | copy-start | bytes 1572868
  432.5 15.7 %copy-start.4 = (f32[1024]{0:T(1024)S(1)}, f32[1024]{0:T(1024)}, u32[]{:S(2)}) copy-start(f32[1024]{0:T(1024)} %param.13) | copy-start | bytes 12292
Sparse Core Ops, SparseCore 0:
  9.6 65.4 all-gather.2
